TPU v7x, 32 devices: a whole 2x2x4 slice. The times are simulated.
32 devices in a mesh: fields: 2 (over x), seq: 8 (over z, y), head: 2 (over core).
Axes of the slice: x: 2, y: 2, z: 4, core: 2. Of those that a mesh axis runs over, the one named last changes fastest.
Arguments:
- tokens: bfloat16 [65536, 512], P(('fields', 'seq')), parts along dimension 0, may hold values from -6 to 6
- norm_gain: float32 [512], replicated, may hold values from 0.1 to 1.9
- coarse_gain: float32 [512], replicated, may hold values from 0.25 to 2.5
- w_query: bfloat16 [512, 512], P(None, 'head'), may hold values from -0.25 to 0.25
- w_key: bfloat16 [512, 512], P(None, 'head'), may hold values from -0.25 to 0.25
- w_value: bfloat16 [512, 512], P(None, 'head'), may hold values from -0.25 to 0.25
- w_out: bfloat16 [512, 512], replicated, may hold values from -0.25 to 0.25
- score_scale: float32 [8], P('head'), may hold values from 1 to 40, as said below
Outputs:
- attn_out: bfloat16 [65536, 512], P(('fields', 'seq'), 'head'), parts along dimension 0
There are 2 independent parts, one for each index of `fields`. A program takes and returns all parts, laid end to end along the dimension named above; an argument that names none is the same for every part. Nothing has to cross between parts.
Inputs may be any that keep to these rules, and one draw needn't show every extreme that they name: `score_scale`: per-head score temperature.
All inputs are finite; a program needn't handle non-finite values.
Results may differ from a plain program's by a relative error of at most 0.0035.
The roundings to bfloat16 on the way count: a program that leaves them out, or rounds other values in their place, can miss the bound.
Values may be sent and summed in bfloat16 or wider, within the bound.
No kernel may reach another device: no remote copies, remote signals or barrier semaphores. Data moves between devices by JAX's collectives and lax.ppermute only.
A program may use at most 64 MiB of HBM per device.

v0:
```python
import jax
import jax.numpy as jnp
from jax import lax
from jax.sharding import PartitionSpec as P

HEAD_DIM = 64
WINDOW = 256
POOL = 1024
QB = 512


def with_halo(block, sides, width):
    for axis, dim in sides:
        count = lax.axis_size(axis)
        forward = [(i, i + 1) for i in range(count - 1)]
        backward = [(target, source) for source, target in forward]
        low = lax.ppermute(
            lax.slice_in_dim(block, block.shape[dim] - width, None, axis=dim), axis, forward
        )
        high = lax.ppermute(lax.slice_in_dim(block, 0, width, axis=dim), axis, backward)
        block = jnp.concatenate([low, block, high], axis=dim)
    return block


def rms_rows(matrix, scaling):
    return matrix * lax.rsqrt(jnp.mean(matrix * matrix, axis=-1, keepdims=True) + 1e-05) * scaling


def unit_heads(matrix, head_count):
    split = matrix.reshape(matrix.shape[0], head_count, HEAD_DIM)
    return split * lax.rsqrt(jnp.mean(split * split, axis=-1, keepdims=True) + 1e-06)


def body(tokens, norm_gain, coarse_gain, w_query, w_key, w_value, w_out, score_scale):
    tok_count = tokens.shape[0]
    full_width = tokens.shape[1]
    local_heads = score_scale.shape[0]
    width = local_heads * HEAD_DIM
    seq_index = lax.axis_index("seq")
    total_tokens = tok_count * lax.axis_size("seq")
    normed = rms_rows(tokens.astype(jnp.float32), norm_gain).astype(jnp.bfloat16)
    factor = (score_scale * HEAD_DIM ** (-0.5))[None, :, None]
    queries = (
        unit_heads(jnp.dot(normed, w_query, preferred_element_type=jnp.float32), local_heads)
        * factor
    ).astype(jnp.bfloat16)
    key_rows = unit_heads(
        jnp.dot(normed, w_key, preferred_element_type=jnp.float32), local_heads
    ).astype(jnp.bfloat16)
    value_rows = jnp.dot(normed, w_value, preferred_element_type=jnp.float32).astype(jnp.bfloat16)
    stacked = jnp.stack([key_rows.reshape(tok_count, width), value_rows])
    extended = with_halo(stacked, (("seq", 1),), WINDOW)
    extended = extended.reshape(2, tok_count + 2 * WINDOW, local_heads, HEAD_DIM)
    normed_kept = lax.optimization_barrier(normed)
    pooled = jnp.mean(
        normed_kept.astype(jnp.float32).reshape(tok_count // POOL, POOL, full_width), axis=1
    )
    coarse = rms_rows(pooled, coarse_gain).astype(jnp.bfloat16)
    coarse_keys = unit_heads(
        jnp.dot(coarse, w_key, preferred_element_type=jnp.float32), local_heads
    ).astype(jnp.bfloat16)
    coarse_values = jnp.dot(coarse, w_value, preferred_element_type=jnp.float32).astype(
        jnp.bfloat16
    )
    coarse_stack = jnp.stack([coarse_keys.reshape(coarse.shape[0], width), coarse_values])
    coarse_all = lax.all_gather(coarse_stack, "seq", axis=1, tiled=True)
    coarse_all = coarse_all.reshape(2, coarse_all.shape[1], local_heads, HEAD_DIM)
    span = QB + 2 * WINDOW
    offsets = (
        jnp.arange(QB, dtype=jnp.int32)[:, None]
        - jnp.arange(span, dtype=jnp.int32)[None, :]
        + WINDOW
    )
    near = jnp.abs(offsets) <= WINDOW

    def one_block(block_id):
        row_start = block_id * QB
        block_queries = lax.dynamic_slice_in_dim(queries, row_start, QB, 0)
        block_keys = lax.dynamic_slice_in_dim(extended[0], row_start, span, 0)
        block_values = lax.dynamic_slice_in_dim(extended[1], row_start, span, 0)
        band = jnp.einsum(
            "qhd,khd->hqk", block_queries, block_keys, preferred_element_type=jnp.float32
        )
        positions = seq_index * tok_count + row_start + jnp.arange(span, dtype=jnp.int32) - WINDOW
        inside = (positions >= 0) & (positions < total_tokens)
        band = jnp.where(near[None] & inside[None, None, :], band, -1e30)
        far = jnp.einsum(
            "qhd,khd->hqk", block_queries, coarse_all[0], preferred_element_type=jnp.float32
        )
        peak = jnp.maximum(
            jnp.max(band, axis=-1, keepdims=True), jnp.max(far, axis=-1, keepdims=True)
        )
        band_exp = jnp.exp(band - peak)
        far_exp = jnp.exp(far - peak)
        total = jnp.sum(band_exp, axis=-1, keepdims=True) + jnp.sum(far_exp, axis=-1, keepdims=True)
        band_weights = (band_exp / total).astype(jnp.bfloat16)
        far_weights = (far_exp / total).astype(jnp.bfloat16)
        mixed = jnp.einsum(
            "hqk,khd->qhd", band_weights, block_values, preferred_element_type=jnp.float32
        )
        mixed = mixed + jnp.einsum(
            "hqk,khd->qhd", far_weights, coarse_all[1], preferred_element_type=jnp.float32
        )
        return mixed.astype(jnp.bfloat16).reshape(QB, width)

    attended = lax.map(one_block, jnp.arange(tok_count // QB, dtype=jnp.int32)).reshape(
        tok_count, width
    )
    head_index = lax.axis_index("head")
    own_rows = lax.dynamic_slice_in_dim(w_out, head_index * width, width, 0)
    partial_out = jnp.dot(attended, own_rows, preferred_element_type=jnp.float32)
    summed = lax.psum_scatter(partial_out, "head", scatter_dimension=1, tiled=True)
    return summed.astype(jnp.bfloat16)


def solution(mesh):
    return jax.shard_map(
        body,
        mesh=mesh,
        in_specs=(
            P(("fields", "seq"), None),
            P(),
            P(),
            P(None, "head"),
            P(None, "head"),
            P(None, "head"),
            P(),
            P("head"),
        ),
        out_specs=P(("fields", "seq"), "head"),
        check_vma=False,
    )
```

profile of v0, /device:TPU:0, one launch (start us, length us, event | category | flops | bytes accessed | tf_op | source)
XLA Modules:
  0.0 215.3 jit_solution(245271120795114434)
XLA Ops:
  6.5 3.2 %fusion.30 = f32[4096]{0:T(1024)S(1)} fusion(bf16[4096,512]{1,0:T(8,128)(2,1)} %param.10), kind=kLoop, calls=%fused_computation.40 | loop fusion | flops 6287360 | bytes 4210688 | tf_op jit(solution)/shard_map/reduce_sum | solution.py:26
  10.1 1.1 fusion.32
  11.2 1.4 bitcast_reduce_fusion
  12.7 1.3 fusion.33
  14.4 0.7 pad_maximum_fusion.2
  15.5 4.9 %collective-permute-start = (bf16[2,256,256]{1,2,0:T(8,128)(2,1)}, bf16[2,256,256]{1,2,0:T(8,128)(2,1)S(1)}, u32[]{:S(2)}, u32[]{:S(2)}) collective-permute-start(bf16[2,256,256]{1,2,0:T(8,128)(2,1)} %get-tuple-element.173), channel_id=1, source_target_pairs={{0,2},{2,4},{4,6},{6,8},{8,10},{10,12},{12,14},{1,3},{3,5},{5,7},{... | collective-permute-start | bytes 786440 | tf_op jit(solution)/shard_map/ppermute | solution.py:17
  20.4 1.3 collective-permute-start.1
  22.9 3.6 %multiply_reduce_fusion = (f32[4096,4]{0,1:T(4,128)S(1)}, f32[4096,256]{0,1:T(8,128)S(1)}) fusion(bf16[4096,512]{1,0:T(8,128)(2,1)} %copy-done.1, bf16[512,256]{1,0:T(8,128)(2,1)S(1)} %copy-done.5), kind=kOutput, calls=%fused_computation.51 | convolution fusion | flops 1075822592 | bytes 8716288 | tf_op jit(solution)/shard_map/dot_general | solution.py:44
  26.6 1.9 multiply_convert_fusion
  28.5 1.1 fusion.35
  29.6 32.9 %all_gather.3 = bf16[2,32,256]{2,0,1:T(2,128)(2,1)S(1)} all-gather(bf16[2,4,256]{2,0,1:T(2,128)(2,1)S(1)} %copy.19), channel_id=1, replica_groups=mesh['fields'=2,'seq'=8,'head'=2] {'seq'}, dimensions={1}, use_global_device_ids=true | all-gather | bytes 36864 | tf_op jit(solution)/shard_map/all_gather | solution.py:66
  62.7 3.6 %pad_maximum_fusion = bf16[2,4608,256]{1,2,0:T(8,128)(2,1)} fusion(bf16[2,256,256]{1,2,0:T(8,128)(2,1)} %collective-permute-done.1, bf16[1,4096,256]{1,2,0:T(8,128)(2,1)} %copy-done.3, bf16[1,4096,256]{1,2,0:T(8,128)(2,1)S(1)} %bitcast.76, bf16[2,256,256]{1,2,0:T(8,128)(2,1)S(1)} %collective-permute-done), kind=kLoop, calls=%fused_computation.46 | loop fusion | flops 18874368 | bytes 9437184 | tf_op jit(solution)/shard_map/concatenate | solution.py:21
  66.4 114.6 %while.13 = (s32[]{:T(128)}, bf16[8,512,256]{2,1,0:T(8,128)(2,1)}, bf16[2,4608,4,64]{1,3,2,0:T(8,128)(2,1)}, s32[8]{0:T(128)S(1)}, s32[]{:T(128)}, /*index=5*/bf...) while((s32[]{:T(128)}, bf16[8,512,256]{2,1,0:T(8,128)(2,1)}, ...), condition=%wide.region_11.12_spmd.clone, body=%wide.region_6.11_spmd.clone.sunk | while | flops 575800320 | bytes 41618152 | solution.py:106
  68.2 2.8 %fusion.67 = (bf16[1,4608,4,64]{1,3,2,0:T(8,128)(2,1)S(1)}, bf16[1,4608,4,64]{1,3,2,0:T(8,128)(2,1)S(1)}) fusion(bf16[2,4608,4,64]{1,3,2,0:T(8,128)(2,1)} %get-tuple-element.262), kind=kLoop, calls=%fused_computation.71.clone.1 | loop fusion | bytes 9437184 | tf_op jit(solution)/shard_map/while/body/eval_jaxpr/slice | solution.py:80
  71.1 2.5 %select_reduce_fusion.2 = (f32[4,512]{1,0:T(4,128)S(1)}, f32[4,512,1024]{2,1,0:T(8,128)S(1)}) fusion(pred[512,1024]{1,0:T(8,128)(4,1)S(1)} %fusion.66, bf16[1,4608,4,64]{1,3,2,0:T(8,128)(2,1)S(1)} %get-tuple-element.230, s32[]{:T(128)S(6)} %select_n.44, bf16[4096,4,64]{0,2,1:T(8,128)(2,1)} %get-tuple-element.265, s32[]{:T(128)S(6)} %select_n.45), kind=kOutput, calls=%fused_computation.3.clone.1 | convolution fusion | flops 272627712 | bytes 9707528 | tf_op jit(solution)/shard_map/while/body/eval_jaxpr/qhd,khd->hqk/dot_general | solution.py:81
  73.5 1.1 fusion.68
  74.8 2.3 %fusion.69 = f32[4,512]{1,0:T(4,128)S(1)} fusion(f32[4,512,1024]{2,1,0:T(8,128)S(1)} %get-tuple-element.231, f32[4,512]{1,0:T(4,128)S(1)} %max.13, pred[512,1024]{1,0:T(8,128)(4,1)S(1)} %fusion.66), kind=kLoop, calls=%fused_computation.4.clone.1 | loop fusion | flops 6289408 | bytes 8929280 | tf_op jit(solution)/shard_map/while/body/eval_jaxpr/reduce_sum | solution.py:95
  77.0 2.5 %fusion.71 = f32[512,4,64]{0,2,1:T(8,128)S(1)} fusion(f32[4,512,1024]{2,1,0:T(8,128)S(1)} %get-tuple-element.231, f32[4,512]{1,0:T(4,128)S(1)} %add.173, f32[4,512]{1,0:T(4,128)S(1)} %max.13, pred[512,1024]{1,0:T(8,128)(4,1)S(1)} %fusion.66, bf16[1,4608,4,64]{1,3,2,0:T(8,128)(2,1)S(1)} %get-tuple-element.235, s32[]{:T(128)S(6)} %select_n.44), kind=kOutput, calls=%fused_computation.8.clone.1 | convolution fusion | flops 276824064 | bytes 9977860 | tf_op jit(solution)/shard_map/while/body/eval_jaxpr/hqk,khd->qhd/dot_general | solution.py:98
  80.0 0.7 constant_dynamic-update-slice_fusion.2
  82.5 2.8 %fusion.67 = (bf16[1,4608,4,64]{1,3,2,0:T(8,128)(2,1)S(1)}, bf16[1,4608,4,64]{1,3,2,0:T(8,128)(2,1)S(1)}) fusion(bf16[2,4608,4,64]{1,3,2,0:T(8,128)(2,1)} %get-tuple-element.262), kind=kLoop, calls=%fused_computation.71.clone.1 | loop fusion | bytes 9437184 | tf_op jit(solution)/shard_map/while/body/eval_jaxpr/slice | solution.py:80
  85.4 2.5 %select_reduce_fusion.2 = (f32[4,512]{1,0:T(4,128)S(1)}, f32[4,512,1024]{2,1,0:T(8,128)S(1)}) fusion(pred[512,1024]{1,0:T(8,128)(4,1)S(1)} %fusion.66, bf16[1,4608,4,64]{1,3,2,0:T(8,128)(2,1)S(1)} %get-tuple-element.230, s32[]{:T(128)S(6)} %select_n.44, bf16[4096,4,64]{0,2,1:T(8,128)(2,1)} %get-tuple-element.265, s32[]{:T(128)S(6)} %select_n.45), kind=kOutput, calls=%fused_computation.3.clone.1 | convolution fusion | flops 272627712 | bytes 9707528 | tf_op jit(solution)/shard_map/while/body/eval_jaxpr/qhd,khd->hqk/dot_general | solution.py:81
  87.9 1.1 fusion.68
  89.1 2.3 %fusion.69 = f32[4,512]{1,0:T(4,128)S(1)} fusion(f32[4,512,1024]{2,1,0:T(8,128)S(1)} %get-tuple-element.231, f32[4,512]{1,0:T(4,128)S(1)} %max.13, pred[512,1024]{1,0:T(8,128)(4,1)S(1)} %fusion.66), kind=kLoop, calls=%fused_computation.4.clone.1 | loop fusion | flops 6289408 | bytes 8929280 | tf_op jit(solution)/shard_map/while/body/eval_jaxpr/reduce_sum | solution.py:95
  91.4 2.5 %fusion.71 = f32[512,4,64]{0,2,1:T(8,128)S(1)} fusion(f32[4,512,1024]{2,1,0:T(8,128)S(1)} %get-tuple-element.231, f32[4,512]{1,0:T(4,128)S(1)} %add.173, f32[4,512]{1,0:T(4,128)S(1)} %max.13, pred[512,1024]{1,0:T(8,128)(4,1)S(1)} %fusion.66, bf16[1,4608,4,64]{1,3,2,0:T(8,128)(2,1)S(1)} %get-tuple-element.235, s32[]{:T(128)S(6)} %select_n.44), kind=kOutput, calls=%fused_computation.8.clone.1 | convolution fusion | flops 276824064 | bytes 9977860 | tf_op jit(solution)/shard_map/while/body/eval_jaxpr/hqk,khd->qhd/dot_general | solution.py:98
  94.3 0.7 constant_dynamic-update-slice_fusion.2
  96.9 2.8 %fusion.67 = (bf16[1,4608,4,64]{1,3,2,0:T(8,128)(2,1)S(1)}, bf16[1,4608,4,64]{1,3,2,0:T(8,128)(2,1)S(1)}) fusion(bf16[2,4608,4,64]{1,3,2,0:T(8,128)(2,1)} %get-tuple-element.262), kind=kLoop, calls=%fused_computation.71.clone.1 | loop fusion | bytes 9437184 | tf_op jit(solution)/shard_map/while/body/eval_jaxpr/slice | solution.py:80
  99.7 2.5 %select_reduce_fusion.2 = (f32[4,512]{1,0:T(4,128)S(1)}, f32[4,512,1024]{2,1,0:T(8,128)S(1)}) fusion(pred[512,1024]{1,0:T(8,128)(4,1)S(1)} %fusion.66, bf16[1,4608,4,64]{1,3,2,0:T(8,128)(2,1)S(1)} %get-tuple-element.230, s32[]{:T(128)S(6)} %select_n.44, bf16[4096,4,64]{0,2,1:T(8,128)(2,1)} %get-tuple-element.265, s32[]{:T(128)S(6)} %select_n.45), kind=kOutput, calls=%fused_computation.3.clone.1 | convolution fusion | flops 272627712 | bytes 9707528 | tf_op jit(solution)/shard_map/while/body/eval_jaxpr/qhd,khd->hqk/dot_general | solution.py:81
  102.2 1.1 fusion.68
  103.4 2.3 %fusion.69 = f32[4,512]{1,0:T(4,128)S(1)} fusion(f32[4,512,1024]{2,1,0:T(8,128)S(1)} %get-tuple-element.231, f32[4,512]{1,0:T(4,128)S(1)} %max.13, pred[512,1024]{1,0:T(8,128)(4,1)S(1)} %fusion.66), kind=kLoop, calls=%fused_computation.4.clone.1 | loop fusion | flops 6289408 | bytes 8929280 | tf_op jit(solution)/shard_map/while/body/eval_jaxpr/reduce_sum | solution.py:95
  105.7 2.5 %fusion.71 = f32[512,4,64]{0,2,1:T(8,128)S(1)} fusion(f32[4,512,1024]{2,1,0:T(8,128)S(1)} %get-tuple-element.231, f32[4,512]{1,0:T(4,128)S(1)} %add.173, f32[4,512]{1,0:T(4,128)S(1)} %max.13, pred[512,1024]{1,0:T(8,128)(4,1)S(1)} %fusion.66, bf16[1,4608,4,64]{1,3,2,0:T(8,128)(2,1)S(1)} %get-tuple-element.235, s32[]{:T(128)S(6)} %select_n.44), kind=kOutput, calls=%fused_computation.8.clone.1 | convolution fusion | flops 276824064 | bytes 9977860 | tf_op jit(solution)/shard_map/while/body/eval_jaxpr/hqk,khd->qhd/dot_general | solution.py:98
  108.6 0.7 constant_dynamic-update-slice_fusion.2
  111.2 2.8 %fusion.67 = (bf16[1,4608,4,64]{1,3,2,0:T(8,128)(2,1)S(1)}, bf16[1,4608,4,64]{1,3,2,0:T(8,128)(2,1)S(1)}) fusion(bf16[2,4608,4,64]{1,3,2,0:T(8,128)(2,1)} %get-tuple-element.262), kind=kLoop, calls=%fused_computation.71.clone.1 | loop fusion | bytes 9437184 | tf_op jit(solution)/shard_map/while/body/eval_jaxpr/slice | solution.py:80
  114.0 2.5 %select_reduce_fusion.2 = (f32[4,512]{1,0:T(4,128)S(1)}, f32[4,512,1024]{2,1,0:T(8,128)S(1)}) fusion(pred[512,1024]{1,0:T(8,128)(4,1)S(1)} %fusion.66, bf16[1,4608,4,64]{1,3,2,0:T(8,128)(2,1)S(1)} %get-tuple-element.230, s32[]{:T(128)S(6)} %select_n.44, bf16[4096,4,64]{0,2,1:T(8,128)(2,1)} %get-tuple-element.265, s32[]{:T(128)S(6)} %select_n.45), kind=kOutput, calls=%fused_computation.3.clone.1 | convolution fusion | flops 272627712 | bytes 9707528 | tf_op jit(solution)/shard_map/while/body/eval_jaxpr/qhd,khd->hqk/dot_general | solution.py:81
  116.5 1.1 fusion.68
  117.7 2.3 %fusion.69 = f32[4,512]{1,0:T(4,128)S(1)} fusion(f32[4,512,1024]{2,1,0:T(8,128)S(1)} %get-tuple-element.231, f32[4,512]{1,0:T(4,128)S(1)} %max.13, pred[512,1024]{1,0:T(8,128)(4,1)S(1)} %fusion.66), kind=kLoop, calls=%fused_computation.4.clone.1 | loop fusion | flops 6289408 | bytes 8929280 | tf_op jit(solution)/shard_map/while/body/eval_jaxpr/reduce_sum | solution.py:95
  120.0 2.5 %fusion.71 = f32[512,4,64]{0,2,1:T(8,128)S(1)} fusion(f32[4,512,1024]{2,1,0:T(8,128)S(1)} %get-tuple-element.231, f32[4,512]{1,0:T(4,128)S(1)} %add.173, f32[4,512]{1,0:T(4,128)S(1)} %max.13, pred[512,1024]{1,0:T(8,128)(4,1)S(1)} %fusion.66, bf16[1,4608,4,64]{1,3,2,0:T(8,128)(2,1)S(1)} %get-tuple-element.235, s32[]{:T(128)S(6)} %select_n.44), kind=kOutput, calls=%fused_computation.8.clone.1 | convolution fusion | flops 276824064 | bytes 9977860 | tf_op jit(solution)/shard_map/while/body/eval_jaxpr/hqk,khd->qhd/dot_general | solution.py:98
  122.9 0.7 constant_dynamic-update-slice_fusion.2
  125.5 2.8 %fusion.67 = (bf16[1,4608,4,64]{1,3,2,0:T(8,128)(2,1)S(1)}, bf16[1,4608,4,64]{1,3,2,0:T(8,128)(2,1)S(1)}) fusion(bf16[2,4608,4,64]{1,3,2,0:T(8,128)(2,1)} %get-tuple-element.262), kind=kLoop, calls=%fused_computation.71.clone.1 | loop fusion | bytes 9437184 | tf_op jit(solution)/shard_map/while/body/eval_jaxpr/slice | solution.py:80
  128.3 2.5 %select_reduce_fusion.2 = (f32[4,512]{1,0:T(4,128)S(1)}, f32[4,512,1024]{2,1,0:T(8,128)S(1)}) fusion(pred[512,1024]{1,0:T(8,128)(4,1)S(1)} %fusion.66, bf16[1,4608,4,64]{1,3,2,0:T(8,128)(2,1)S(1)} %get-tuple-element.230, s32[]{:T(128)S(6)} %select_n.44, bf16[4096,4,64]{0,2,1:T(8,128)(2,1)} %get-tuple-element.265, s32[]{:T(128)S(6)} %select_n.45), kind=kOutput, calls=%fused_computation.3.clone.1 | convolution fusion | flops 272627712 | bytes 9707528 | tf_op jit(solution)/shard_map/while/body/eval_jaxpr/qhd,khd->hqk/dot_general | solution.py:81
  130.8 1.1 fusion.68
  132.0 2.3 %fusion.69 = f32[4,512]{1,0:T(4,128)S(1)} fusion(f32[4,512,1024]{2,1,0:T(8,128)S(1)} %get-tuple-element.231, f32[4,512]{1,0:T(4,128)S(1)} %max.13, pred[512,1024]{1,0:T(8,128)(4,1)S(1)} %fusion.66), kind=kLoop, calls=%fused_computation.4.clone.1 | loop fusion | flops 6289408 | bytes 8929280 | tf_op jit(solution)/shard_map/while/body/eval_jaxpr/reduce_sum | solution.py:95
  134.3 2.5 %fusion.71 = f32[512,4,64]{0,2,1:T(8,128)S(1)} fusion(f32[4,512,1024]{2,1,0:T(8,128)S(1)} %get-tuple-element.231, f32[4,512]{1,0:T(4,128)S(1)} %add.173, f32[4,512]{1,0:T(4,128)S(1)} %max.13, pred[512,1024]{1,0:T(8,128)(4,1)S(1)} %fusion.66, bf16[1,4608,4,64]{1,3,2,0:T(8,128)(2,1)S(1)} %get-tuple-element.235, s32[]{:T(128)S(6)} %select_n.44), kind=kOutput, calls=%fused_computation.8.clone.1 | convolution fusion | flops 276824064 | bytes 9977860 | tf_op jit(solution)/shard_map/while/body/eval_jaxpr/hqk,khd->qhd/dot_general | solution.py:98
  137.3 0.7 constant_dynamic-update-slice_fusion.2
  139.8 2.8 %fusion.67 = (bf16[1,4608,4,64]{1,3,2,0:T(8,128)(2,1)S(1)}, bf16[1,4608,4,64]{1,3,2,0:T(8,128)(2,1)S(1)}) fusion(bf16[2,4608,4,64]{1,3,2,0:T(8,128)(2,1)} %get-tuple-element.262), kind=kLoop, calls=%fused_computation.71.clone.1 | loop fusion | bytes 9437184 | tf_op jit(solution)/shard_map/while/body/eval_jaxpr/slice | solution.py:80
  142.7 2.5 %select_reduce_fusion.2 = (f32[4,512]{1,0:T(4,128)S(1)}, f32[4,512,1024]{2,1,0:T(8,128)S(1)}) fusion(pred[512,1024]{1,0:T(8,128)(4,1)S(1)} %fusion.66, bf16[1,4608,4,64]{1,3,2,0:T(8,128)(2,1)S(1)} %get-tuple-element.230, s32[]{:T(128)S(6)} %select_n.44, bf16[4096,4,64]{0,2,1:T(8,128)(2,1)} %get-tuple-element.265, s32[]{:T(128)S(6)} %select_n.45), kind=kOutput, calls=%fused_computation.3.clone.1 | convolution fusion | flops 272627712 | bytes 9707528 | tf_op jit(solution)/shard_map/while/body/eval_jaxpr/qhd,khd->hqk/dot_general | solution.py:81
  145.1 1.1 fusion.68
  146.4 2.3 %fusion.69 = f32[4,512]{1,0:T(4,128)S(1)} fusion(f32[4,512,1024]{2,1,0:T(8,128)S(1)} %get-tuple-element.231, f32[4,512]{1,0:T(4,128)S(1)} %max.13, pred[512,1024]{1,0:T(8,128)(4,1)S(1)} %fusion.66), kind=kLoop, calls=%fused_computation.4.clone.1 | loop fusion | flops 6289408 | bytes 8929280 | tf_op jit(solution)/shard_map/while/body/eval_jaxpr/reduce_sum | solution.py:95
  148.6 2.5 %fusion.71 = f32[512,4,64]{0,2,1:T(8,128)S(1)} fusion(f32[4,512,1024]{2,1,0:T(8,128)S(1)} %get-tuple-element.231, f32[4,512]{1,0:T(4,128)S(1)} %add.173, f32[4,512]{1,0:T(4,128)S(1)} %max.13, pred[512,1024]{1,0:T(8,128)(4,1)S(1)} %fusion.66, bf16[1,4608,4,64]{1,3,2,0:T(8,128)(2,1)S(1)} %get-tuple-element.235, s32[]{:T(128)S(6)} %select_n.44), kind=kOutput, calls=%fused_computation.8.clone.1 | convolution fusion | flops 276824064 | bytes 9977860 | tf_op jit(solution)/shard_map/while/body/eval_jaxpr/hqk,khd->qhd/dot_general | solution.py:98
  151.6 0.7 constant_dynamic-update-slice_fusion.2
  154.1 2.8 %fusion.67 = (bf16[1,4608,4,64]{1,3,2,0:T(8,128)(2,1)S(1)}, bf16[1,4608,4,64]{1,3,2,0:T(8,128)(2,1)S(1)}) fusion(bf16[2,4608,4,64]{1,3,2,0:T(8,128)(2,1)} %get-tuple-element.262), kind=kLoop, calls=%fused_computation.71.clone.1 | loop fusion | bytes 9437184 | tf_op jit(solution)/shard_map/while/body/eval_jaxpr/slice | solution.py:80
  157.0 2.5 %select_reduce_fusion.2 = (f32[4,512]{1,0:T(4,128)S(1)}, f32[4,512,1024]{2,1,0:T(8,128)S(1)}) fusion(pred[512,1024]{1,0:T(8,128)(4,1)S(1)} %fusion.66, bf16[1,4608,4,64]{1,3,2,0:T(8,128)(2,1)S(1)} %get-tuple-element.230, s32[]{:T(128)S(6)} %select_n.44, bf16[4096,4,64]{0,2,1:T(8,128)(2,1)} %get-tuple-element.265, s32[]{:T(128)S(6)} %select_n.45), kind=kOutput, calls=%fused_computation.3.clone.1 | convolution fusion | flops 272627712 | bytes 9707528 | tf_op jit(solution)/shard_map/while/body/eval_jaxpr/qhd,khd->hqk/dot_general | solution.py:81
  159.5 1.1 fusion.68
  160.7 2.3 %fusion.69 = f32[4,512]{1,0:T(4,128)S(1)} fusion(f32[4,512,1024]{2,1,0:T(8,128)S(1)} %get-tuple-element.231, f32[4,512]{1,0:T(4,128)S(1)} %max.13, pred[512,1024]{1,0:T(8,128)(4,1)S(1)} %fusion.66), kind=kLoop, calls=%fused_computation.4.clone.1 | loop fusion | flops 6289408 | bytes 8929280 | tf_op jit(solution)/shard_map/while/body/eval_jaxpr/reduce_sum | solution.py:95
  163.0 2.5 %fusion.71 = f32[512,4,64]{0,2,1:T(8,128)S(1)} fusion(f32[4,512,1024]{2,1,0:T(8,128)S(1)} %get-tuple-element.231, f32[4,512]{1,0:T(4,128)S(1)} %add.173, f32[4,512]{1,0:T(4,128)S(1)} %max.13, pred[512,1024]{1,0:T(8,128)(4,1)S(1)} %fusion.66, bf16[1,4608,4,64]{1,3,2,0:T(8,128)(2,1)S(1)} %get-tuple-element.235, s32[]{:T(128)S(6)} %select_n.44), kind=kOutput, calls=%fused_computation.8.clone.1 | convolution fusion | flops 276824064 | bytes 9977860 | tf_op jit(solution)/shard_map/while/body/eval_jaxpr/hqk,khd->qhd/dot_general | solution.py:98
  165.9 0.7 constant_dynamic-update-slice_fusion.2
  168.5 2.8 %fusion.67 = (bf16[1,4608,4,64]{1,3,2,0:T(8,128)(2,1)S(1)}, bf16[1,4608,4,64]{1,3,2,0:T(8,128)(2,1)S(1)}) fusion(bf16[2,4608,4,64]{1,3,2,0:T(8,128)(2,1)} %get-tuple-element.262), kind=kLoop, calls=%fused_computation.71.clone.1 | loop fusion | bytes 9437184 | tf_op jit(solution)/shard_map/while/body/eval_jaxpr/slice | solution.py:80
  171.3 2.5 %select_reduce_fusion.2 = (f32[4,512]{1,0:T(4,128)S(1)}, f32[4,512,1024]{2,1,0:T(8,128)S(1)}) fusion(pred[512,1024]{1,0:T(8,128)(4,1)S(1)} %fusion.66, bf16[1,4608,4,64]{1,3,2,0:T(8,128)(2,1)S(1)} %get-tuple-element.230, s32[]{:T(128)S(6)} %select_n.44, bf16[4096,4,64]{0,2,1:T(8,128)(2,1)} %get-tuple-element.265, s32[]{:T(128)S(6)} %select_n.45), kind=kOutput, calls=%fused_computation.3.clone.1 | convolution fusion | flops 272627712 | bytes 9707528 | tf_op jit(solution)/shard_map/while/body/eval_jaxpr/qhd,khd->hqk/dot_general | solution.py:81
  173.8 1.1 fusion.68
  175.0 2.3 %fusion.69 = f32[4,512]{1,0:T(4,128)S(1)} fusion(f32[4,512,1024]{2,1,0:T(8,128)S(1)} %get-tuple-element.231, f32[4,512]{1,0:T(4,128)S(1)} %max.13, pred[512,1024]{1,0:T(8,128)(4,1)S(1)} %fusion.66), kind=kLoop, calls=%fused_computation.4.clone.1 | loop fusion | flops 6289408 | bytes 8929280 | tf_op jit(solution)/shard_map/while/body/eval_jaxpr/reduce_sum | solution.py:95
  177.3 2.5 %fusion.71 = f32[512,4,64]{0,2,1:T(8,128)S(1)} fusion(f32[4,512,1024]{2,1,0:T(8,128)S(1)} %get-tuple-element.231, f32[4,512]{1,0:T(4,128)S(1)} %add.173, f32[4,512]{1,0:T(4,128)S(1)} %max.13, pred[512,1024]{1,0:T(8,128)(4,1)S(1)} %fusion.66, bf16[1,4608,4,64]{1,3,2,0:T(8,128)(2,1)S(1)} %get-tuple-element.235, s32[]{:T(128)S(6)} %select_n.44), kind=kOutput, calls=%fused_computation.8.clone.1 | convolution fusion | flops 276824064 | bytes 9977860 | tf_op jit(solution)/shard_map/while/body/eval_jaxpr/hqk,khd->qhd/dot_general | solution.py:98
  180.2 0.7 constant_dynamic-update-slice_fusion.2
  181.0 6.1 %fusion.36 = f32[4096,512]{1,0:T(8,128)} fusion(bf16[4096,256]{1,0:T(8,128)(2,1)} %bitcast.78, bf16[512,512]{1,0:T(8,128)(2,1)S(1)} %copy-done, s32[]{:T(128)S(6)} %select_n.23), kind=kOutput, calls=%fused_computation.56 | convolution fusion | flops 1073741824 | bytes 10747908 | tf_op jit(solution)/shard_map/dot_general | solution.py:111
  187.0 17.7 %reduce-scatter.2.cloned.1.call-done = f32[4096,256]{1,0:T(8,128)} async-done(((f32[4096,512]{1,0:T(8,128)}), f32[4096,256]{1,0:T(8,128)}) %reduce-scatter.2.cloned.1.call-update) | async-done | bytes 4194320 | tf_op jit(solution)/shard_map/reduce_scatter | solution.py:112
  204.7 3.7 %convert_element_type.64 = bf16[4096,256]{1,0:T(8,128)(2,1)} convert(f32[4096,256]{1,0:T(8,128)} %reduce-scatter.2.cloned.1.call-done) | non-fusion elementwise | flops 1048576 | bytes 6291456 | tf_op jit(solution)/shard_map/convert_element_type | solution.py:113
  (109 shorter events, 15.2 us)
Async XLA Ops:
  6.5 174.4 %copy-start = (bf16[512,512]{1,0:T(8,128)(2,1)S(1)}, bf16[512,512]{1,0:T(8,128)(2,1)}, u32[]{:S(2)}) copy-start(bf16[512,512]{1,0:T(8,128)(2,1)} %param.16) | copy-start | bytes 1572868
  6.5 3.3 %copy-start.6 = (f32[512]{0:T(512)S(1)}, f32[512]{0:T(512)}, u32[]{:S(2)}) copy-start(f32[512]{0:T(512)} %param.11) | copy-start | bytes 6148
  6.5 198.2 %reduce-scatter.2.cloned.1.call-start = ((), (), s32[]{:S(2)}) async-start(), calls=%async_computation.1 | async-start | bytes 12582912 | tf_op jit(solution)/shard_map/reduce_scatter | solution.py:112
  6.5 3.5 %copy-start.2 = (bf16[4096,512]{1,0:T(8,128)(2,1)S(1)}, bf16[4096,512]{1,0:T(8,128)(2,1)}, u32[]{:S(2)}) copy-start(bf16[4096,512]{1,0:T(8,128)(2,1)} %param.10) | copy-start | bytes 12582916
  10.1 1.1 copy-start.4
  11.2 10.5 %copy-start.1 = (bf16[4096,512]{1,0:T(8,128)(2,1)}, bf16[4096,512]{1,0:T(8,128)(2,1)S(1)}, u32[]{:S(2)}) copy-start(bf16[4096,512]{1,0:T(8,128)(2,1)S(1)} %fusion.32) | copy-start | bytes 12582916
  11.2 1.5 copy-start.7
  14.0 1.5 copy-start.3
  14.4 8.0 %copy-start.8 = (f32[512]{0:T(512)S(1)}, f32[512]{0:T(512)}, u32[]{:S(2)}) copy-start(f32[512]{0:T(512)} %param.12) | copy-start | bytes 6148
  14.4 8.5 %copy-start.5 = (bf16[512,256]{1,0:T(8,128)(2,1)S(1)}, bf16[512,256]{1,0:T(8,128)(2,1)}, u32[]{:S(2)}) copy-start(bf16[512,256]{1,0:T(8,128)(2,1)} %param.13) | copy-start | bytes 786436
  15.5 47.2 %collective-permute-start = (bf16[2,256,256]{1,2,0:T(8,128)(2,1)}, bf16[2,256,256]{1,2,0:T(8,128)(2,1)S(1)}, u32[]{:S(2)}, u32[]{:S(2)}) collective-permute-start(bf16[2,256,256]{1,2,0:T(8,128)(2,1)} %get-tuple-element.173), channel_id=1, source_target_pairs={{0,2},{2,4},{4,6},{6,8},{8,10},{10,12},{12,14},{1,3},{3,5},{5,7},{... | collective-permute-start | bytes 786440 | tf_op jit(solution)/shard_map/ppermute | solution.py:17
  20.4 42.4 %collective-permute-start.1 = (bf16[2,256,256]{1,2,0:T(8,128)(2,1)S(1)}, bf16[2,256,256]{1,2,0:T(8,128)(2,1)}, u32[]{:S(2)}, u32[]{:S(2)}) collective-permute-start(bf16[2,256,256]{1,2,0:T(8,128)(2,1)S(1)} %get-tuple-element.174), channel_id=1, source_target_pairs={{2,0},{4,2},{6,4},{8,6},{10,8},{12,10},{14,12},{3,1},{5,3},{7,5},{... | collective-permute-start | bytes 786440 | tf_op jit(solution)/shard_map/ppermute | solution.py:20
  22.9 3.6 %copy-start.9 = (f32[4]{0:T(128)S(1)}, f32[4]{0:T(128)}, u32[]{:S(2)}) copy-start(f32[4]{0:T(128)} %param.17) | copy-start | bytes 52
Sparse Core Ops, SparseCore 0:
  187.2 17.5 reduce-scatter.1
where the time goes:
time: 216 us; the launch traced here: 215 us
  matrix products  64.9 us (30%)
  other arithmetic  37.8 us (17%)
  local copies, waits for them, and re-layouts  36 us (17%)
  blocking collectives  32.9 us (15%)
  waiting for transfers between devices  17.7 us (8%)
  between operations  13.6 us (6%)
  starting transfers between devices  6.17 us (3%)
  loops' own time  6.09 us (3%)
    all_gather x1, blocking collectives, body(): coarse_all = lax.all_gather(coarse_stack, 'seq', axis=1, tiled=True)  32.9 us
    slice x8, local copies, waits for them, and re-layouts, one_block(): block_values = lax.dynamic_slice_in_dim(extended[1], row_start, span, 0)  22.7 us
    dot_general x8, matrix products, one_block(): jnp.einsum('hqk,khd->qhd', band_weights, block_values, preferred_element_...  20.1 us
    dot_general x8, matrix products, one_block(): jnp.einsum('qhd,khd->hqk', block_queries, block_keys, preferred_element_t...  19.9 us
    reduce_sum x8, other arithmetic, one_block(): jnp.sum(band_exp, axis=-1, keepdims=True)  18.2 us
    reduce_scatter x1, waiting for transfers between devices, body(): lax.psum_scatter(partial_out, 'head', scatter_dimension=1, tiled=True)  17.7 us
    dot_general x8, matrix products, one_block(): jnp.einsum('qhd,khd->hqk', block_queries, coarse_all[0], preferred_elemen...  9.05 us
    dynamic_update_slice x16, local copies, waits for them, and re-layouts, body(): lax.map(one_block, jnp.arange(tok_count // QB, dtype=jnp.int32))  6.92 us
  transfers between devices with their start and end apart: 3, of which 1 were waited for; matrix products, arithmetic and copies ran while one was open for 4% of the time, Pallas kernels for 0%

commit v1 on v0

--- a/solution.py
+++ b/solution.py
@@ -63,7 +63,34 @@
         jnp.bfloat16
     )
     coarse_stack = jnp.stack([coarse_keys.reshape(coarse.shape[0], width), coarse_values])
-    coarse_all = lax.all_gather(coarse_stack, "seq", axis=1, tiled=True)
+    f_next = lax.axis_size("seq")
+    last = lax.axis_index("seq")
+    column = []
+    k_now, answer, local_part = (f_next, last, coarse_stack.shape[1])
+    for t in range(k_now):
+        column.append((t, (t + 1) % k_now))
+    block_list = []
+    for t in range(k_now):
+        block_list.append((t, (t - 1) % k_now))
+    coarse_all = jnp.zeros(
+        (*coarse_stack.shape[:1], k_now * local_part, *coarse_stack.shape[1 + 1 :]),
+        coarse_stack.dtype,
+    )
+    coarse_all = lax.dynamic_update_slice_in_dim(
+        coarse_all, coarse_stack, answer * local_part, axis=1
+    )
+    now = moved = coarse_stack
+    earlier = k_now // 2
+    for at in range(1, earlier + 1):
+        now = lax.ppermute(now, "seq", column)
+        coarse_all = lax.dynamic_update_slice_in_dim(
+            coarse_all, now, (answer - at) % k_now * local_part, axis=1
+        )
+        if at < k_now - earlier:
+            moved = lax.ppermute(moved, "seq", block_list)
+            coarse_all = lax.dynamic_update_slice_in_dim(
+                coarse_all, moved, (answer + at) % k_now * local_part, axis=1
+            )
     coarse_all = coarse_all.reshape(2, coarse_all.shape[1], local_heads, HEAD_DIM)
     span = QB + 2 * WINDOW
     offsets = (

time: 216 us -> 206 us (0.954)
  blocking collectives: 32.9 us -> 0 us
  starting transfers between devices: 6.17 us -> 19.4 us
  waiting for transfers between devices: 17.7 us -> 23.5 us
    all_gather x1 -> x0, blocking collectives: 32.9 us -> none  [body(): coarse_all = lax.all_gather(coarse_stack, 'seq', axis=1, tiled=True)]
    ppermute x0 -> x7, starting transfers between devices: none -> 16.8 us  [the longest x3 11.1 us: body(): moved = lax.ppermute(moved, 'seq', block_list)]
    ppermute x0 -> x7, waiting for transfers between devices: none -> 9.27 us  [the longest x4 9.26 us: body(): now = lax.ppermute(now, 'seq', column)]
    ppermute x1, starting transfers between devices: 4.87 us -> 1.29 us  [with_halo(): lax.ppermute(lax.slice_in_dim(block, block.shape[dim] - width, None, axis...]
    reduce_scatter x1, waiting for transfers between devices: 17.7 us -> 14.2 us  [body(): lax.psum_scatter(partial_out, 'head', scatter_dimension=1, tiled=True)]
    dot_general x1, matrix products: 1.41 us -> 3.6 us  [body(): jnp.dot(normed, w_key, preferred_element_type=jnp.float32)]
  transfers between devices with their start and end apart: 3 -> 10, of which waited for: 1 -> 4; matrix products, arithmetic and copies ran while one was open for 4% -> 6% of each run, Pallas kernels for 0% -> 0%
where the time goes in v1:
time: 206 us; the launch traced here: 205 us
  matrix products  66.2 us (32%)
  other arithmetic  38.3 us (19%)
  local copies, waits for them, and re-layouts  37.8 us (18%)
  waiting for transfers between devices  23.5 us (11%)
  starting transfers between devices  19.4 us (9%)
  between operations  13.7 us (7%)
  loops' own time  6.1 us (3%)
    slice x8, local copies, waits for them, and re-layouts, one_block(): block_values = lax.dynamic_slice_in_dim(extended[1], row_start, span, 0)  22.7 us
    dot_general x8, matrix products, one_block(): jnp.einsum('hqk,khd->qhd', band_weights, block_values, preferred_element_...  20.1 us
    dot_general x8, matrix products, one_block(): jnp.einsum('qhd,khd->hqk', block_queries, block_keys, preferred_element_t...  19.9 us
    reduce_sum x8, other arithmetic, one_block(): jnp.sum(band_exp, axis=-1, keepdims=True)  18.2 us
    reduce_scatter x1, waiting for transfers between devices, body(): lax.psum_scatter(partial_out, 'head', scatter_dimension=1, tiled=True)  14.2 us
    ppermute x3, starting transfers between devices, body(): moved = lax.ppermute(moved, 'seq', block_list)  11.1 us
    ppermute x4, waiting for transfers between devices, body(): now = lax.ppermute(now, 'seq', column)  9.26 us
    dot_general x8, matrix products, one_block(): jnp.einsum('qhd,khd->hqk', block_queries, coarse_all[0], preferred_elemen...  9.06 us
  transfers between devices with their start and end apart: 10, of which 4 were waited for; matrix products, arithmetic and copies ran while one was open for 6% of the time, Pallas kernels for 0%

profile of v1, /device:TPU:0, one launch (start us, length us, event | category | flops | bytes accessed | tf_op | source)
XLA Modules:
  0.0 205.0 jit_solution(9854560529704901598)
XLA Ops:
  6.5 3.2 %fusion.30 = f32[4096]{0:T(1024)S(1)} fusion(bf16[4096,512]{1,0:T(8,128)(2,1)} %param.10), kind=kLoop, calls=%fused_computation.40 | loop fusion | flops 6287360 | bytes 4210688 | tf_op jit(solution)/shard_map/reduce_sum | solution.py:26
  10.1 1.1 fusion.32
  11.2 1.9 copy-done.1
  14.8 3.0 %collective-permute-start.2 = (bf16[2,4,256]{2,1,0:T(4,128)(2,1)S(1)}, bf16[2,4,256]{2,1,0:T(4,128)(2,1)S(1)}, u32[]{:S(2)}, u32[]{:S(2)}) collective-permute-start(bf16[2,4,256]{2,1,0:T(4,128)(2,1)S(1)} %get-tuple-element.161), channel_id=1, source_target_pairs={{0,2},{2,4},{4,6},{6,8},{8,10},{10,12},{12,14},{14,0},{1,3},{3,5},... | collective-permute-start | bytes 12296 | tf_op jit(solution)/shard_map/ppermute | solution.py:85
  17.9 3.1 %collective-permute-start.3 = (bf16[2,4,256]{2,1,0:T(4,128)(2,1)S(1)}, bf16[2,4,256]{2,1,0:T(4,128)(2,1)S(1)}, u32[]{:S(2)}, u32[]{:S(2)}) collective-permute-start(bf16[2,4,256]{2,1,0:T(4,128)(2,1)S(1)} %get-tuple-element.161), channel_id=1, source_target_pairs={{0,14},{2,0},{4,2},{6,4},{8,6},{10,8},{12,10},{14,12},{1,15},{3,1}... | collective-permute-start | bytes 12296 | tf_op jit(solution)/shard_map/ppermute | solution.py:90
  21.0 3.6 %bitcast_reduce_fusion = (f32[4096,4]{0,1:T(4,128)S(1)}, f32[4096,256]{0,1:T(8,128)S(1)}) fusion(bf16[4096,512]{1,0:T(8,128)(2,1)} %copy-done.1, bf16[512,256]{1,0:T(8,128)(2,1)S(1)} %copy-done.5), kind=kOutput, calls=%fused_computation.49 | convolution fusion | flops 1075822592 | bytes 8716288 | tf_op jit(solution)/shard_map/dot_general | solution.py:48
  24.6 1.4 fusion.33
  26.4 1.1 pad_maximum_fusion.2
  27.4 1.3 collective-permute-start
  28.7 1.3 collective-permute-start.1
  30.1 3.5 %multiply_reduce_fusion = (f32[4096,4]{0,1:T(4,128)S(1)}, f32[4096,256]{0,1:T(8,128)S(1)}) fusion(bf16[4096,512]{1,0:T(8,128)(2,1)} %copy-done.1, bf16[512,256]{1,0:T(8,128)(2,1)S(1)} %copy-done.6), kind=kOutput, calls=%fused_computation.51 | convolution fusion | flops 1075822592 | bytes 8716288 | tf_op jit(solution)/shard_map/dot_general | solution.py:44
  33.7 1.9 multiply_convert_fusion
  35.6 2.6 %collective-permute-start.4 = (bf16[2,4,256]{2,1,0:T(4,128)(2,1)S(1)}, bf16[2,4,256]{2,1,0:T(4,128)(2,1)S(1)}, u32[]{:S(2)}, u32[]{:S(2)}) collective-permute-start(bf16[2,4,256]{2,1,0:T(4,128)(2,1)S(1)} %collective-permute-done.2), channel_id=1, source_target_pairs={{0,2},{2,4},{4,6},{6,8},{8,10},{10,12},{12,14},{14,0},{1,3},{3,5},... | collective-permute-start | bytes 12296 | tf_op jit(solution)/shard_map/ppermute | solution.py:85
  38.3 3.3 %collective-permute-start.5 = (bf16[2,4,256]{2,1,0:T(4,128)(2,1)S(1)}, bf16[2,4,256]{2,1,0:T(4,128)(2,1)S(1)}, u32[]{:S(2)}, u32[]{:S(2)}) collective-permute-start(bf16[2,4,256]{2,1,0:T(4,128)(2,1)S(1)} %collective-permute-done.3), channel_id=1, source_target_pairs={{0,14},{2,0},{4,2},{6,4},{8,6},{10,8},{12,10},{14,12},{1,15},{3,1}... | collective-permute-start | bytes 12296 | tf_op jit(solution)/shard_map/ppermute | solution.py:90
  41.6 1.5 collective-permute-done.4
  43.1 4.8 %collective-permute-start.7 = (bf16[2,4,256]{2,1,0:T(4,128)(2,1)S(1)}, bf16[2,4,256]{2,1,0:T(4,128)(2,1)S(1)}, u32[]{:S(2)}, u32[]{:S(2)}) collective-permute-start(bf16[2,4,256]{2,1,0:T(4,128)(2,1)S(1)} %collective-permute-done.5), channel_id=1, source_target_pairs={{0,14},{2,0},{4,2},{6,4},{8,6},{10,8},{12,10},{14,12},{1,15},{3,1}... | collective-permute-start | bytes 12296 | tf_op jit(solution)/shard_map/ppermute | solution.py:90
  47.9 1.5 collective-permute-done.6
  49.4 6.3 %collective-permute-done.8 = bf16[2,4,256]{2,1,0:T(4,128)(2,1)S(1)} collective-permute-done((bf16[2,4,256]{2,1,0:T(4,128)(2,1)S(1)}, bf16[2,4,256]{2,1,0:T(4,128)(2,1)S(1)}, u32[]{:S(2)}, u32[]{:S(2)}) %collective-permute-start.8) | collective-permute-done | bytes 4128 | tf_op jit(solution)/shard_map/ppermute | solution.py:85
  55.8 3.6 %pad_maximum_fusion = bf16[2,4608,256]{1,2,0:T(8,128)(2,1)} fusion(bf16[2,256,256]{1,2,0:T(8,128)(2,1)} %collective-permute-done.1, bf16[1,4096,256]{1,2,0:T(8,128)(2,1)} %copy-done.4, bf16[1,4096,256]{1,2,0:T(8,128)(2,1)S(1)} %bitcast.74, bf16[2,256,256]{1,2,0:T(8,128)(2,1)S(1)} %collective-permute-done), kind=kLoop, calls=%fused_computation.46 | loop fusion | flops 18874368 | bytes 9437184 | tf_op jit(solution)/shard_map/concatenate | solution.py:21
  59.5 114.6 %while.13 = (s32[]{:T(128)}, bf16[8,512,256]{2,1,0:T(8,128)(2,1)}, bf16[2,4608,4,64]{1,3,2,0:T(8,128)(2,1)}, s32[8]{0:T(128)S(1)}, s32[]{:T(128)}, /*index=5*/bf...) while((s32[]{:T(128)}, bf16[8,512,256]{2,1,0:T(8,128)(2,1)}, ...), condition=%wide.region_11.12_spmd.clone, body=%wide.region_6.11_spmd.clone.sunk | while | flops 575800320 | bytes 41618152 | solution.py:133
  61.3 2.8 %fusion.67 = (bf16[1,4608,4,64]{1,3,2,0:T(8,128)(2,1)S(1)}, bf16[1,4608,4,64]{1,3,2,0:T(8,128)(2,1)S(1)}) fusion(bf16[2,4608,4,64]{1,3,2,0:T(8,128)(2,1)} %get-tuple-element.250), kind=kLoop, calls=%fused_computation.79.clone.1 | loop fusion | bytes 9437184 | tf_op jit(solution)/shard_map/while/body/eval_jaxpr/slice | solution.py:107
  64.2 2.5 %select_reduce_fusion.2 = (f32[4,512]{1,0:T(4,128)S(1)}, f32[4,512,1024]{2,1,0:T(8,128)S(1)}) fusion(pred[512,1024]{1,0:T(8,128)(4,1)S(1)} %fusion.66, bf16[1,4608,4,64]{1,3,2,0:T(8,128)(2,1)S(1)} %get-tuple-element.218, s32[]{:T(128)S(6)} %select_n.114, bf16[4096,4,64]{0,2,1:T(8,128)(2,1)} %get-tuple-element.253, s32[]{:T(128)S(6)} %select_n.115), kind=kOutput, calls=%fused_computation.3.clone.1 | convolution fusion | flops 272627712 | bytes 9707528 | tf_op jit(solution)/shard_map/while/body/eval_jaxpr/qhd,khd->hqk/dot_general | solution.py:108
  66.7 1.1 fusion.68
  67.9 2.3 %fusion.69 = f32[4,512]{1,0:T(4,128)S(1)} fusion(f32[4,512,1024]{2,1,0:T(8,128)S(1)} %get-tuple-element.219, f32[4,512]{1,0:T(4,128)S(1)} %max.13, pred[512,1024]{1,0:T(8,128)(4,1)S(1)} %fusion.66), kind=kLoop, calls=%fused_computation.4.clone.1 | loop fusion | flops 6289408 | bytes 8929280 | tf_op jit(solution)/shard_map/while/body/eval_jaxpr/reduce_sum | solution.py:122
  70.2 2.5 %fusion.71 = f32[512,4,64]{0,2,1:T(8,128)S(1)} fusion(f32[4,512,1024]{2,1,0:T(8,128)S(1)} %get-tuple-element.219, f32[4,512]{1,0:T(4,128)S(1)} %add.250, f32[4,512]{1,0:T(4,128)S(1)} %max.13, pred[512,1024]{1,0:T(8,128)(4,1)S(1)} %fusion.66, bf16[1,4608,4,64]{1,3,2,0:T(8,128)(2,1)S(1)} %get-tuple-element.223, s32[]{:T(128)S(6)} %select_n.114), kind=kOutput, calls=%fused_computation.8.clone.1 | convolution fusion | flops 276824064 | bytes 9977860 | tf_op jit(solution)/shard_map/while/body/eval_jaxpr/hqk,khd->qhd/dot_general | solution.py:125
  73.1 0.7 constant_dynamic-update-slice_fusion.10
  75.6 2.8 %fusion.67 = (bf16[1,4608,4,64]{1,3,2,0:T(8,128)(2,1)S(1)}, bf16[1,4608,4,64]{1,3,2,0:T(8,128)(2,1)S(1)}) fusion(bf16[2,4608,4,64]{1,3,2,0:T(8,128)(2,1)} %get-tuple-element.250), kind=kLoop, calls=%fused_computation.79.clone.1 | loop fusion | bytes 9437184 | tf_op jit(solution)/shard_map/while/body/eval_jaxpr/slice | solution.py:107
  78.5 2.5 %select_reduce_fusion.2 = (f32[4,512]{1,0:T(4,128)S(1)}, f32[4,512,1024]{2,1,0:T(8,128)S(1)}) fusion(pred[512,1024]{1,0:T(8,128)(4,1)S(1)} %fusion.66, bf16[1,4608,4,64]{1,3,2,0:T(8,128)(2,1)S(1)} %get-tuple-element.218, s32[]{:T(128)S(6)} %select_n.114, bf16[4096,4,64]{0,2,1:T(8,128)(2,1)} %get-tuple-element.253, s32[]{:T(128)S(6)} %select_n.115), kind=kOutput, calls=%fused_computation.3.clone.1 | convolution fusion | flops 272627712 | bytes 9707528 | tf_op jit(solution)/shard_map/while/body/eval_jaxpr/qhd,khd->hqk/dot_general | solution.py:108
  81.0 1.1 fusion.68
  82.2 2.3 %fusion.69 = f32[4,512]{1,0:T(4,128)S(1)} fusion(f32[4,512,1024]{2,1,0:T(8,128)S(1)} %get-tuple-element.219, f32[4,512]{1,0:T(4,128)S(1)} %max.13, pred[512,1024]{1,0:T(8,128)(4,1)S(1)} %fusion.66), kind=kLoop, calls=%fused_computation.4.clone.1 | loop fusion | flops 6289408 | bytes 8929280 | tf_op jit(solution)/shard_map/while/body/eval_jaxpr/reduce_sum | solution.py:122
  84.5 2.5 %fusion.71 = f32[512,4,64]{0,2,1:T(8,128)S(1)} fusion(f32[4,512,1024]{2,1,0:T(8,128)S(1)} %get-tuple-element.219, f32[4,512]{1,0:T(4,128)S(1)} %add.250, f32[4,512]{1,0:T(4,128)S(1)} %max.13, pred[512,1024]{1,0:T(8,128)(4,1)S(1)} %fusion.66, bf16[1,4608,4,64]{1,3,2,0:T(8,128)(2,1)S(1)} %get-tuple-element.223, s32[]{:T(128)S(6)} %select_n.114), kind=kOutput, calls=%fused_computation.8.clone.1 | convolution fusion | flops 276824064 | bytes 9977860 | tf_op jit(solution)/shard_map/while/body/eval_jaxpr/hqk,khd->qhd/dot_general | solution.py:125
  90.0 2.8 %fusion.67 = (bf16[1,4608,4,64]{1,3,2,0:T(8,128)(2,1)S(1)}, bf16[1,4608,4,64]{1,3,2,0:T(8,128)(2,1)S(1)}) fusion(bf16[2,4608,4,64]{1,3,2,0:T(8,128)(2,1)} %get-tuple-element.250), kind=kLoop, calls=%fused_computation.79.clone.1 | loop fusion | bytes 9437184 | tf_op jit(solution)/shard_map/while/body/eval_jaxpr/slice | solution.py:107
  92.8 2.5 %select_reduce_fusion.2 = (f32[4,512]{1,0:T(4,128)S(1)}, f32[4,512,1024]{2,1,0:T(8,128)S(1)}) fusion(pred[512,1024]{1,0:T(8,128)(4,1)S(1)} %fusion.66, bf16[1,4608,4,64]{1,3,2,0:T(8,128)(2,1)S(1)} %get-tuple-element.218, s32[]{:T(128)S(6)} %select_n.114, bf16[4096,4,64]{0,2,1:T(8,128)(2,1)} %get-tuple-element.253, s32[]{:T(128)S(6)} %select_n.115), kind=kOutput, calls=%fused_computation.3.clone.1 | convolution fusion | flops 272627712 | bytes 9707528 | tf_op jit(solution)/shard_map/while/body/eval_jaxpr/qhd,khd->hqk/dot_general | solution.py:108
  95.3 1.1 fusion.68
  96.5 2.3 %fusion.69 = f32[4,512]{1,0:T(4,128)S(1)} fusion(f32[4,512,1024]{2,1,0:T(8,128)S(1)} %get-tuple-element.219, f32[4,512]{1,0:T(4,128)S(1)} %max.13, pred[512,1024]{1,0:T(8,128)(4,1)S(1)} %fusion.66), kind=kLoop, calls=%fused_computation.4.clone.1 | loop fusion | flops 6289408 | bytes 8929280 | tf_op jit(solution)/shard_map/while/body/eval_jaxpr/reduce_sum | solution.py:122
  98.8 2.5 %fusion.71 = f32[512,4,64]{0,2,1:T(8,128)S(1)} fusion(f32[4,512,1024]{2,1,0:T(8,128)S(1)} %get-tuple-element.219, f32[4,512]{1,0:T(4,128)S(1)} %add.250, f32[4,512]{1,0:T(4,128)S(1)} %max.13, pred[512,1024]{1,0:T(8,128)(4,1)S(1)} %fusion.66, bf16[1,4608,4,64]{1,3,2,0:T(8,128)(2,1)S(1)} %get-tuple-element.223, s32[]{:T(128)S(6)} %select_n.114), kind=kOutput, calls=%fused_computation.8.clone.1 | convolution fusion | flops 276824064 | bytes 9977860 | tf_op jit(solution)/shard_map/while/body/eval_jaxpr/hqk,khd->qhd/dot_general | solution.py:125
  104.3 2.8 %fusion.67 = (bf16[1,4608,4,64]{1,3,2,0:T(8,128)(2,1)S(1)}, bf16[1,4608,4,64]{1,3,2,0:T(8,128)(2,1)S(1)}) fusion(bf16[2,4608,4,64]{1,3,2,0:T(8,128)(2,1)} %get-tuple-element.250), kind=kLoop, calls=%fused_computation.79.clone.1 | loop fusion | bytes 9437184 | tf_op jit(solution)/shard_map/while/body/eval_jaxpr/slice | solution.py:107
  107.1 2.5 %select_reduce_fusion.2 = (f32[4,512]{1,0:T(4,128)S(1)}, f32[4,512,1024]{2,1,0:T(8,128)S(1)}) fusion(pred[512,1024]{1,0:T(8,128)(4,1)S(1)} %fusion.66, bf16[1,4608,4,64]{1,3,2,0:T(8,128)(2,1)S(1)} %get-tuple-element.218, s32[]{:T(128)S(6)} %select_n.114, bf16[4096,4,64]{0,2,1:T(8,128)(2,1)} %get-tuple-element.253, s32[]{:T(128)S(6)} %select_n.115), kind=kOutput, calls=%fused_computation.3.clone.1 | convolution fusion | flops 272627712 | bytes 9707528 | tf_op jit(solution)/shard_map/while/body/eval_jaxpr/qhd,khd->hqk/dot_general | solution.py:108
  109.6 1.1 fusion.68
  110.8 2.3 %fusion.69 = f32[4,512]{1,0:T(4,128)S(1)} fusion(f32[4,512,1024]{2,1,0:T(8,128)S(1)} %get-tuple-element.219, f32[4,512]{1,0:T(4,128)S(1)} %max.13, pred[512,1024]{1,0:T(8,128)(4,1)S(1)} %fusion.66), kind=kLoop, calls=%fused_computation.4.clone.1 | loop fusion | flops 6289408 | bytes 8929280 | tf_op jit(solution)/shard_map/while/body/eval_jaxpr/reduce_sum | solution.py:122
  113.1 2.5 %fusion.71 = f32[512,4,64]{0,2,1:T(8,128)S(1)} fusion(f32[4,512,1024]{2,1,0:T(8,128)S(1)} %get-tuple-element.219, f32[4,512]{1,0:T(4,128)S(1)} %add.250, f32[4,512]{1,0:T(4,128)S(1)} %max.13, pred[512,1024]{1,0:T(8,128)(4,1)S(1)} %fusion.66, bf16[1,4608,4,64]{1,3,2,0:T(8,128)(2,1)S(1)} %get-tuple-element.223, s32[]{:T(128)S(6)} %select_n.114), kind=kOutput, calls=%fused_computation.8.clone.1 | convolution fusion | flops 276824064 | bytes 9977860 | tf_op jit(solution)/shard_map/while/body/eval_jaxpr/hqk,khd->qhd/dot_general | solution.py:125
  118.6 2.8 %fusion.67 = (bf16[1,4608,4,64]{1,3,2,0:T(8,128)(2,1)S(1)}, bf16[1,4608,4,64]{1,3,2,0:T(8,128)(2,1)S(1)}) fusion(bf16[2,4608,4,64]{1,3,2,0:T(8,128)(2,1)} %get-tuple-element.250), kind=kLoop, calls=%fused_computation.79.clone.1 | loop fusion | bytes 9437184 | tf_op jit(solution)/shard_map/while/body/eval_jaxpr/slice | solution.py:107
  121.5 2.5 %select_reduce_fusion.2 = (f32[4,512]{1,0:T(4,128)S(1)}, f32[4,512,1024]{2,1,0:T(8,128)S(1)}) fusion(pred[512,1024]{1,0:T(8,128)(4,1)S(1)} %fusion.66, bf16[1,4608,4,64]{1,3,2,0:T(8,128)(2,1)S(1)} %get-tuple-element.218, s32[]{:T(128)S(6)} %select_n.114, bf16[4096,4,64]{0,2,1:T(8,128)(2,1)} %get-tuple-element.253, s32[]{:T(128)S(6)} %select_n.115), kind=kOutput, calls=%fused_computation.3.clone.1 | convolution fusion | flops 272627712 | bytes 9707528 | tf_op jit(solution)/shard_map/while/body/eval_jaxpr/qhd,khd->hqk/dot_general | solution.py:108
  124.0 1.1 fusion.68
  125.2 2.3 %fusion.69 = f32[4,512]{1,0:T(4,128)S(1)} fusion(f32[4,512,1024]{2,1,0:T(8,128)S(1)} %get-tuple-element.219, f32[4,512]{1,0:T(4,128)S(1)} %max.13, pred[512,1024]{1,0:T(8,128)(4,1)S(1)} %fusion.66), kind=kLoop, calls=%fused_computation.4.clone.1 | loop fusion | flops 6289408 | bytes 8929280 | tf_op jit(solution)/shard_map/while/body/eval_jaxpr/reduce_sum | solution.py:122
  127.5 2.5 %fusion.71 = f32[512,4,64]{0,2,1:T(8,128)S(1)} fusion(f32[4,512,1024]{2,1,0:T(8,128)S(1)} %get-tuple-element.219, f32[4,512]{1,0:T(4,128)S(1)} %add.250, f32[4,512]{1,0:T(4,128)S(1)} %max.13, pred[512,1024]{1,0:T(8,128)(4,1)S(1)} %fusion.66, bf16[1,4608,4,64]{1,3,2,0:T(8,128)(2,1)S(1)} %get-tuple-element.223, s32[]{:T(128)S(6)} %select_n.114), kind=kOutput, calls=%fused_computation.8.clone.1 | convolution fusion | flops 276824064 | bytes 9977860 | tf_op jit(solution)/shard_map/while/body/eval_jaxpr/hqk,khd->qhd/dot_general | solution.py:125
  132.9 2.8 %fusion.67 = (bf16[1,4608,4,64]{1,3,2,0:T(8,128)(2,1)S(1)}, bf16[1,4608,4,64]{1,3,2,0:T(8,128)(2,1)S(1)}) fusion(bf16[2,4608,4,64]{1,3,2,0:T(8,128)(2,1)} %get-tuple-element.250), kind=kLoop, calls=%fused_computation.79.clone.1 | loop fusion | bytes 9437184 | tf_op jit(solution)/shard_map/while/body/eval_jaxpr/slice | solution.py:107
  135.8 2.5 %select_reduce_fusion.2 = (f32[4,512]{1,0:T(4,128)S(1)}, f32[4,512,1024]{2,1,0:T(8,128)S(1)}) fusion(pred[512,1024]{1,0:T(8,128)(4,1)S(1)} %fusion.66, bf16[1,4608,4,64]{1,3,2,0:T(8,128)(2,1)S(1)} %get-tuple-element.218, s32[]{:T(128)S(6)} %select_n.114, bf16[4096,4,64]{0,2,1:T(8,128)(2,1)} %get-tuple-element.253, s32[]{:T(128)S(6)} %select_n.115), kind=kOutput, calls=%fused_computation.3.clone.1 | convolution fusion | flops 272627712 | bytes 9707528 | tf_op jit(solution)/shard_map/while/body/eval_jaxpr/qhd,khd->hqk/dot_general | solution.py:108
  138.3 1.1 fusion.68
  139.5 2.3 %fusion.69 = f32[4,512]{1,0:T(4,128)S(1)} fusion(f32[4,512,1024]{2,1,0:T(8,128)S(1)} %get-tuple-element.219, f32[4,512]{1,0:T(4,128)S(1)} %max.13, pred[512,1024]{1,0:T(8,128)(4,1)S(1)} %fusion.66), kind=kLoop, calls=%fused_computation.4.clone.1 | loop fusion | flops 6289408 | bytes 8929280 | tf_op jit(solution)/shard_map/while/body/eval_jaxpr/reduce_sum | solution.py:122
  141.8 2.5 %fusion.71 = f32[512,4,64]{0,2,1:T(8,128)S(1)} fusion(f32[4,512,1024]{2,1,0:T(8,128)S(1)} %get-tuple-element.219, f32[4,512]{1,0:T(4,128)S(1)} %add.250, f32[4,512]{1,0:T(4,128)S(1)} %max.13, pred[512,1024]{1,0:T(8,128)(4,1)S(1)} %fusion.66, bf16[1,4608,4,64]{1,3,2,0:T(8,128)(2,1)S(1)} %get-tuple-element.223, s32[]{:T(128)S(6)} %select_n.114), kind=kOutput, calls=%fused_computation.8.clone.1 | convolution fusion | flops 276824064 | bytes 9977860 | tf_op jit(solution)/shard_map/while/body/eval_jaxpr/hqk,khd->qhd/dot_general | solution.py:125
  147.3 2.8 %fusion.67 = (bf16[1,4608,4,64]{1,3,2,0:T(8,128)(2,1)S(1)}, bf16[1,4608,4,64]{1,3,2,0:T(8,128)(2,1)S(1)}) fusion(bf16[2,4608,4,64]{1,3,2,0:T(8,128)(2,1)} %get-tuple-element.250), kind=kLoop, calls=%fused_computation.79.clone.1 | loop fusion | bytes 9437184 | tf_op jit(solution)/shard_map/while/body/eval_jaxpr/slice | solution.py:107
  150.1 2.5 %select_reduce_fusion.2 = (f32[4,512]{1,0:T(4,128)S(1)}, f32[4,512,1024]{2,1,0:T(8,128)S(1)}) fusion(pred[512,1024]{1,0:T(8,128)(4,1)S(1)} %fusion.66, bf16[1,4608,4,64]{1,3,2,0:T(8,128)(2,1)S(1)} %get-tuple-element.218, s32[]{:T(128)S(6)} %select_n.114, bf16[4096,4,64]{0,2,1:T(8,128)(2,1)} %get-tuple-element.253, s32[]{:T(128)S(6)} %select_n.115), kind=kOutput, calls=%fused_computation.3.clone.1 | convolution fusion | flops 272627712 | bytes 9707528 | tf_op jit(solution)/shard_map/while/body/eval_jaxpr/qhd,khd->hqk/dot_general | solution.py:108
  152.6 1.1 fusion.68
  153.8 2.3 %fusion.69 = f32[4,512]{1,0:T(4,128)S(1)} fusion(f32[4,512,1024]{2,1,0:T(8,128)S(1)} %get-tuple-element.219, f32[4,512]{1,0:T(4,128)S(1)} %max.13, pred[512,1024]{1,0:T(8,128)(4,1)S(1)} %fusion.66), kind=kLoop, calls=%fused_computation.4.clone.1 | loop fusion | flops 6289408 | bytes 8929280 | tf_op jit(solution)/shard_map/while/body/eval_jaxpr/reduce_sum | solution.py:122
  156.1 2.5 %fusion.71 = f32[512,4,64]{0,2,1:T(8,128)S(1)} fusion(f32[4,512,1024]{2,1,0:T(8,128)S(1)} %get-tuple-element.219, f32[4,512]{1,0:T(4,128)S(1)} %add.250, f32[4,512]{1,0:T(4,128)S(1)} %max.13, pred[512,1024]{1,0:T(8,128)(4,1)S(1)} %fusion.66, bf16[1,4608,4,64]{1,3,2,0:T(8,128)(2,1)S(1)} %get-tuple-element.223, s32[]{:T(128)S(6)} %select_n.114), kind=kOutput, calls=%fused_computation.8.clone.1 | convolution fusion | flops 276824064 | bytes 9977860 | tf_op jit(solution)/shard_map/while/body/eval_jaxpr/hqk,khd->qhd/dot_general | solution.py:125
  161.6 2.8 %fusion.67 = (bf16[1,4608,4,64]{1,3,2,0:T(8,128)(2,1)S(1)}, bf16[1,4608,4,64]{1,3,2,0:T(8,128)(2,1)S(1)}) fusion(bf16[2,4608,4,64]{1,3,2,0:T(8,128)(2,1)} %get-tuple-element.250), kind=kLoop, calls=%fused_computation.79.clone.1 | loop fusion | bytes 9437184 | tf_op jit(solution)/shard_map/while/body/eval_jaxpr/slice | solution.py:107
  164.5 2.5 %select_reduce_fusion.2 = (f32[4,512]{1,0:T(4,128)S(1)}, f32[4,512,1024]{2,1,0:T(8,128)S(1)}) fusion(pred[512,1024]{1,0:T(8,128)(4,1)S(1)} %fusion.66, bf16[1,4608,4,64]{1,3,2,0:T(8,128)(2,1)S(1)} %get-tuple-element.218, s32[]{:T(128)S(6)} %select_n.114, bf16[4096,4,64]{0,2,1:T(8,128)(2,1)} %get-tuple-element.253, s32[]{:T(128)S(6)} %select_n.115), kind=kOutput, calls=%fused_computation.3.clone.1 | convolution fusion | flops 272627712 | bytes 9707528 | tf_op jit(solution)/shard_map/while/body/eval_jaxpr/qhd,khd->hqk/dot_general | solution.py:108
  166.9 1.1 fusion.68
  168.2 2.3 %fusion.69 = f32[4,512]{1,0:T(4,128)S(1)} fusion(f32[4,512,1024]{2,1,0:T(8,128)S(1)} %get-tuple-element.219, f32[4,512]{1,0:T(4,128)S(1)} %max.13, pred[512,1024]{1,0:T(8,128)(4,1)S(1)} %fusion.66), kind=kLoop, calls=%fused_computation.4.clone.1 | loop fusion | flops 6289408 | bytes 8929280 | tf_op jit(solution)/shard_map/while/body/eval_jaxpr/reduce_sum | solution.py:122
  170.5 2.5 %fusion.71 = f32[512,4,64]{0,2,1:T(8,128)S(1)} fusion(f32[4,512,1024]{2,1,0:T(8,128)S(1)} %get-tuple-element.219, f32[4,512]{1,0:T(4,128)S(1)} %add.250, f32[4,512]{1,0:T(4,128)S(1)} %max.13, pred[512,1024]{1,0:T(8,128)(4,1)S(1)} %fusion.66, bf16[1,4608,4,64]{1,3,2,0:T(8,128)(2,1)S(1)} %get-tuple-element.223, s32[]{:T(128)S(6)} %select_n.114), kind=kOutput, calls=%fused_computation.8.clone.1 | convolution fusion | flops 276824064 | bytes 9977860 | tf_op jit(solution)/shard_map/while/body/eval_jaxpr/hqk,khd->qhd/dot_general | solution.py:125
  174.1 6.1 %fusion.36 = f32[4096,512]{1,0:T(8,128)} fusion(bf16[4096,256]{1,0:T(8,128)(2,1)} %bitcast.76, bf16[512,512]{1,0:T(8,128)(2,1)S(1)} %copy-done, s32[]{:T(128)S(6)} %select_n.93), kind=kOutput, calls=%fused_computation.56 | convolution fusion | flops 1073741824 | bytes 10747908 | tf_op jit(solution)/shard_map/dot_general | solution.py:138
  180.2 14.2 %reduce-scatter.2.cloned.1.call-done = f32[4096,256]{1,0:T(8,128)} async-done(((f32[4096,512]{1,0:T(8,128)}), f32[4096,256]{1,0:T(8,128)}) %reduce-scatter.2.cloned.1.call-update) | async-done | bytes 4194320 | tf_op jit(solution)/shard_map/reduce_scatter | solution.py:139
  194.4 3.7 %convert_element_type.64 = bf16[4096,256]{1,0:T(8,128)(2,1)} convert(f32[4096,256]{1,0:T(8,128)} %reduce-scatter.2.cloned.1.call-done) | non-fusion elementwise | flops 1048576 | bytes 6291456 | tf_op jit(solution)/shard_map/convert_element_type | solution.py:140
  (131 shorter events, 20.4 us)
Async XLA Ops:
  6.5 167.6 %copy-start = (bf16[512,512]{1,0:T(8,128)(2,1)S(1)}, bf16[512,512]{1,0:T(8,128)(2,1)}, u32[]{:S(2)}) copy-start(bf16[512,512]{1,0:T(8,128)(2,1)} %param.16) | copy-start | bytes 1572868
  6.5 3.3 %copy-start.7 = (f32[512]{0:T(512)S(1)}, f32[512]{0:T(512)}, u32[]{:S(2)}) copy-start(f32[512]{0:T(512)} %param.11) | copy-start | bytes 6148
  6.5 187.9 %reduce-scatter.2.cloned.1.call-start = ((), (), s32[]{:S(2)}) async-start(), calls=%async_computation.1 | async-start | bytes 12582912 | tf_op jit(solution)/shard_map/reduce_scatter | solution.py:139
  6.5 3.5 %copy-start.3 = (bf16[4096,512]{1,0:T(8,128)(2,1)S(1)}, bf16[4096,512]{1,0:T(8,128)(2,1)}, u32[]{:S(2)}) copy-start(bf16[4096,512]{1,0:T(8,128)(2,1)} %param.10) | copy-start | bytes 12582916
  11.2 1.9 copy-start.1
  13.1 0.9 copy-start.5
  13.1 1.0 copy-start.9
  13.1 1.5 copy-start.8
  14.8 9.7 %copy-start.2 = (bf16[4096,512]{1,0:T(8,128)(2,1)S(1)}, bf16[4096,512]{1,0:T(8,128)(2,1)}, u32[]{:S(2)}) copy-start(bf16[4096,512]{1,0:T(8,128)(2,1)} %copy-done.1) | copy-start | bytes 12582916
  14.8 20.8 %collective-permute-start.2 = (bf16[2,4,256]{2,1,0:T(4,128)(2,1)S(1)}, bf16[2,4,256]{2,1,0:T(4,128)(2,1)S(1)}, u32[]{:S(2)}, u32[]{:S(2)}) collective-permute-start(bf16[2,4,256]{2,1,0:T(4,128)(2,1)S(1)} %get-tuple-element.161), channel_id=1, source_target_pairs={{0,2},{2,4},{4,6},{6,8},{8,10},{10,12},{12,14},{14,0},{1,3},{3,5},... | collective-permute-start | bytes 12296 | tf_op jit(solution)/shard_map/ppermute | solution.py:85
  17.9 20.4 %collective-permute-start.3 = (bf16[2,4,256]{2,1,0:T(4,128)(2,1)S(1)}, bf16[2,4,256]{2,1,0:T(4,128)(2,1)S(1)}, u32[]{:S(2)}, u32[]{:S(2)}) collective-permute-start(bf16[2,4,256]{2,1,0:T(4,128)(2,1)S(1)} %get-tuple-element.161), channel_id=1, source_target_pairs={{0,14},{2,0},{4,2},{6,4},{8,6},{10,8},{12,10},{14,12},{1,15},{3,1}... | collective-permute-start | bytes 12296 | tf_op jit(solution)/shard_map/ppermute | solution.py:90
  25.9 1.5 copy-start.4
  26.0 4.1 %copy-start.6 = (bf16[512,256]{1,0:T(8,128)(2,1)S(1)}, bf16[512,256]{1,0:T(8,128)(2,1)}, u32[]{:S(2)}) copy-start(bf16[512,256]{1,0:T(8,128)(2,1)} %param.13) | copy-start | bytes 786436
  27.4 28.4 %collective-permute-start = (bf16[2,256,256]{1,2,0:T(8,128)(2,1)}, bf16[2,256,256]{1,2,0:T(8,128)(2,1)S(1)}, u32[]{:S(2)}, u32[]{:S(2)}) collective-permute-start(bf16[2,256,256]{1,2,0:T(8,128)(2,1)} %get-tuple-element.159), channel_id=1, source_target_pairs={{0,2},{2,4},{4,6},{6,8},{8,10},{10,12},{12,14},{1,3},{3,5},{5,7},{... | collective-permute-start | bytes 786440 | tf_op jit(solution)/shard_map/ppermute | solution.py:17
  28.7 27.1 %collective-permute-start.1 = (bf16[2,256,256]{1,2,0:T(8,128)(2,1)S(1)}, bf16[2,256,256]{1,2,0:T(8,128)(2,1)}, u32[]{:S(2)}, u32[]{:S(2)}) collective-permute-start(bf16[2,256,256]{1,2,0:T(8,128)(2,1)S(1)} %get-tuple-element.160), channel_id=1, source_target_pairs={{2,0},{4,2},{6,4},{8,6},{10,8},{12,10},{14,12},{3,1},{5,3},{7,5},{... | collective-permute-start | bytes 786440 | tf_op jit(solution)/shard_map/ppermute | solution.py:20
  30.1 3.6 %copy-start.10 = (f32[4]{0:T(128)S(1)}, f32[4]{0:T(128)}, u32[]{:S(2)}) copy-start(f32[4]{0:T(128)} %param.17) | copy-start | bytes 52
  35.6 7.4 %collective-permute-start.4 = (bf16[2,4,256]{2,1,0:T(4,128)(2,1)S(1)}, bf16[2,4,256]{2,1,0:T(4,128)(2,1)S(1)}, u32[]{:S(2)}, u32[]{:S(2)}) collective-permute-start(bf16[2,4,256]{2,1,0:T(4,128)(2,1)S(1)} %collective-permute-done.2), channel_id=1, source_target_pairs={{0,2},{2,4},{4,6},{6,8},{8,10},{10,12},{12,14},{14,0},{1,3},{3,5},... | collective-permute-start | bytes 12296 | tf_op jit(solution)/shard_map/ppermute | solution.py:85
  38.3 4.8 %collective-permute-start.5 = (bf16[2,4,256]{2,1,0:T(4,128)(2,1)S(1)}, bf16[2,4,256]{2,1,0:T(4,128)(2,1)S(1)}, u32[]{:S(2)}, u32[]{:S(2)}) collective-permute-start(bf16[2,4,256]{2,1,0:T(4,128)(2,1)S(1)} %collective-permute-done.3), channel_id=1, source_target_pairs={{0,14},{2,0},{4,2},{6,4},{8,6},{10,8},{12,10},{14,12},{1,15},{3,1}... | collective-permute-start | bytes 12296 | tf_op jit(solution)/shard_map/ppermute | solution.py:90
  43.1 6.3 %collective-permute-start.6 = (bf16[2,4,256]{2,1,0:T(4,128)(2,1)S(1)}, bf16[2,4,256]{2,1,0:T(4,128)(2,1)S(1)}, u32[]{:S(2)}, u32[]{:S(2)}) collective-permute-start(bf16[2,4,256]{2,1,0:T(4,128)(2,1)S(1)} %collective-permute-done.4), channel_id=1, source_target_pairs={{0,2},{2,4},{4,6},{6,8},{8,10},{10,12},{12,14},{14,0},{1,3},{3,5},... | collective-permute-start | bytes 12296 | tf_op jit(solution)/shard_map/ppermute | solution.py:85
  43.1 6.3 %collective-permute-start.7 = (bf16[2,4,256]{2,1,0:T(4,128)(2,1)S(1)}, bf16[2,4,256]{2,1,0:T(4,128)(2,1)S(1)}, u32[]{:S(2)}, u32[]{:S(2)}) collective-permute-start(bf16[2,4,256]{2,1,0:T(4,128)(2,1)S(1)} %collective-permute-done.5), channel_id=1, source_target_pairs={{0,14},{2,0},{4,2},{6,4},{8,6},{10,8},{12,10},{14,12},{1,15},{3,1}... | collective-permute-start | bytes 12296 | tf_op jit(solution)/shard_map/ppermute | solution.py:90
  49.4 6.3 %collective-permute-start.8 = (bf16[2,4,256]{2,1,0:T(4,128)(2,1)S(1)}, bf16[2,4,256]{2,1,0:T(4,128)(2,1)S(1)}, u32[]{:S(2)}, u32[]{:S(2)}) collective-permute-start(bf16[2,4,256]{2,1,0:T(4,128)(2,1)S(1)} %collective-permute-done.6), channel_id=1, source_target_pairs={{0,2},{2,4},{4,6},{6,8},{8,10},{10,12},{12,14},{14,0},{1,3},{3,5},... | collective-permute-start | bytes 12296 | tf_op jit(solution)/shard_map/ppermute | solution.py:85
Sparse Core Ops, SparseCore 0:
  180.3 14.0 reduce-scatter.1
